TPU v7x, 32 devices: a whole 2x2x4 slice. The times are simulated.
32 devices in a mesh: seq: 16 (over z, y, core), wgt: 2 (over x).
Axes of the slice: x: 2, y: 2, z: 4, core: 2. Of those that a mesh axis runs over, the one named last changes fastest.
Arguments:
- hidden: bfloat16 [6144, 5376], P('seq', 'wgt'), may hold values from -6 to 6
- q_weight: bfloat16 [2, 5376, 2048], P(None, 'seq', 'wgt'), may hold values from -448 to 448, as said below
- k_weight: bfloat16 [2, 5376, 1024], P(None, 'seq', 'wgt'), may hold values from -448 to 448, as said below
- v_weight: bfloat16 [2, 5376, 1024], P(None, 'seq', 'wgt'), may hold values from -448 to 448, as said below
- o_weight: bfloat16 [2, 2048, 5376], P(None, 'seq', 'wgt'), may hold values from -448 to 448, as said below
- q_scale: int32 [2, 42, 16], P(None, None, 'wgt'), may hold values from 113 to 117
- k_scale: int32 [2, 42, 8], P(None, None, 'wgt'), may hold values from 113 to 117
- v_scale: int32 [2, 42, 8], P(None, None, 'wgt'), may hold values from 113 to 117
- o_scale: int32 [2, 16, 42], replicated, may hold values from 113 to 117
- in_gain: float32 [2, 5376], replicated, may hold values from 0.5 to 1.5
- post_gain: float32 [2, 5376], P(None, 'wgt'), may hold values from 0.5 to 1.5
- q_gain: float32 [2, 128], replicated, may hold values from 0.1 to 1.9
- k_gain: float32 [2, 128], replicated, may hold values from 0.1 to 1.9
- windows: int32 [2], replicated, may hold values from 512 to 1024, as said below
Outputs:
- state: bfloat16 [6144, 5376], P('seq', 'wgt')
Inputs may be any that keep to these rules, and one draw needn't show every extreme that they name: `q_weight`: every entry is a finite value of the e4m3 floating-point format: sign, 3 mantissa bits, exponents of that format. `k_weight`: every entry is a finite value of the e4m3 floating-point format. `v_weight`: every entry is a finite value of the e4m3 floating-point format. `o_weight`: every entry is a finite value of the e4m3 floating-point format. `windows`: one layer's window is exactly 1024.
All inputs are finite; a program needn't handle non-finite values.
Results may differ from a plain program's by a relative error of at most 0.0095.
Values may be sent and summed in bfloat16 or wider, within the bound.
No kernel may reach another device: no remote copies, remote signals or barrier semaphores. Data moves between devices by JAX's collectives and lax.ppermute only.
A program may use at most 192 MiB of HBM per device.

v0:
```python
import jax
import jax.numpy as jnp
from jax import lax
from jax.sharding import PartitionSpec as P

HD = 128
BLOCK = 128
WINDOW = 1024
LAYERS = 2
eps = 1e-06
query_scale = 168.0 ** (-0.5)
rope_base = 10000.0


def passed_along(array, axis, by):
    size = lax.axis_size(axis)
    pairs = [(i, i + by) for i in range(size) if 0 <= i + by < size]
    return lax.ppermute(array, axis, pairs)


def rmsnorm(values, gain):
    return values * lax.rsqrt(jnp.mean(values * values, axis=-1, keepdims=True) + eps) * gain


def rotate(values, position):
    half = values.shape[-1] // 2
    inverse = rope_base ** (-jnp.arange(half, dtype=jnp.float32) * 2.0 / values.shape[-1])
    angles = position.astype(jnp.float32)[:, None] * inverse[None, :]
    cosine = jnp.cos(angles)[:, None, :]
    sine = jnp.sin(angles)[:, None, :]
    first = values[..., :half]
    second = values[..., half:]
    return jnp.concatenate(
        [first * cosine - second * sine, second * cosine + first * sine], axis=-1
    )


def expand_scales(scale_codes):
    factor = jnp.exp2(scale_codes.astype(jnp.float32) - 127.0)
    return jnp.repeat(jnp.repeat(factor, BLOCK, axis=0), BLOCK, axis=1).astype(jnp.bfloat16)


def per_device(
    hidden,
    q_weight,
    k_weight,
    v_weight,
    o_weight,
    q_scale,
    k_scale,
    v_scale,
    o_scale,
    in_gain,
    post_gain,
    q_gain,
    k_gain,
    windows,
):
    local_rows = hidden.shape[0]
    width_share = hidden.shape[1]
    model_width = in_gain.shape[1]
    seq_index = lax.axis_index("seq")
    column_offset = lax.axis_index("wgt") * width_share
    halo_count = -(-(WINDOW - 1) // local_rows)
    position = seq_index * local_rows + jnp.arange(local_rows, dtype=jnp.int32)
    key_position = (
        seq_index * local_rows
        - halo_count * local_rows
        + jnp.arange((halo_count + 1) * local_rows, dtype=jnp.int32)
    )
    gap = position[:, None] - key_position[None, :]
    columns = column_offset + jnp.arange(width_share, dtype=jnp.int32)
    pick = (
        (columns // BLOCK)[None, :] == jnp.arange(model_width // BLOCK, dtype=jnp.int32)[:, None]
    ).astype(jnp.float32)
    gathered = (
        lax.all_gather(q_weight, "seq", axis=1, tiled=True),
        lax.all_gather(k_weight, "seq", axis=1, tiled=True),
        lax.all_gather(v_weight, "seq", axis=1, tiled=True),
        lax.all_gather(o_weight, "seq", axis=1, tiled=True),
    )
    state = hidden
    for layer_idx in range(LAYERS):
        outgoing = state
        arriving = lax.all_gather(outgoing, "wgt", axis=1, tiled=True)
        normed = rmsnorm(arriving.astype(jnp.float32), in_gain[layer_idx]).astype(jnp.bfloat16)
        tables = (
            expand_scales(q_scale[layer_idx]),
            expand_scales(k_scale[layer_idx]),
            expand_scales(v_scale[layer_idx]),
        )
        o_factor = jnp.exp2(o_scale[layer_idx].astype(jnp.float32) - 127.0)
        o_columns = jnp.dot(o_factor, pick, precision=lax.Precision.HIGHEST)
        o_table = jnp.repeat(o_columns, BLOCK, axis=0).astype(jnp.bfloat16)
        queries = jnp.dot(
            normed, gathered[0][layer_idx] * tables[0], preferred_element_type=jnp.float32
        )
        key_part = jnp.dot(
            normed, gathered[1][layer_idx] * tables[1], preferred_element_type=jnp.float32
        )
        value_part = jnp.dot(
            normed, gathered[2][layer_idx] * tables[2], preferred_element_type=jnp.float32
        )
        queries = (
            rotate(rmsnorm(queries.reshape(local_rows, -1, HD), q_gain[layer_idx]), position)
            * query_scale
        ).astype(jnp.bfloat16)
        key_heads = rotate(
            rmsnorm(key_part.reshape(local_rows, -1, HD), k_gain[layer_idx]), position
        ).astype(jnp.bfloat16)
        key_flat = key_heads.reshape(local_rows, -1)
        value_flat = value_part.astype(jnp.bfloat16)
        earlier = []
        for distance in range(1, halo_count + 1):
            earlier.insert(0, passed_along((key_flat, value_flat), "seq", distance))
        kv_local = key_flat.shape[1] // HD
        groups = queries.shape[1] // kv_local
        all_keys = jnp.concatenate([item[0] for item in earlier] + [key_flat], axis=0).reshape(
            -1, kv_local, HD
        )
        all_values = jnp.concatenate([item[1] for item in earlier] + [value_flat], axis=0).reshape(
            -1, kv_local, HD
        )
        grouped = queries.reshape(local_rows, kv_local, groups, HD)
        scores = jnp.einsum("qkgd,skd->kgqs", grouped, all_keys, preferred_element_type=jnp.float32)
        allowed = (key_position[None, :] >= 0) & (gap >= 0) & (gap < windows[layer_idx])
        scores = jnp.where(allowed, scores, -1e30)
        top = jnp.max(scores, axis=-1, keepdims=True)
        expval = jnp.exp(scores - top)
        weights = (expval / jnp.sum(expval, axis=-1, keepdims=True)).astype(jnp.bfloat16)
        mixed = jnp.einsum(
            "kgqs,skd->qkgd", weights, all_values, preferred_element_type=jnp.float32
        )
        mixed = mixed.reshape(local_rows, -1).astype(jnp.bfloat16)
        mixed_full = lax.all_gather(mixed, "wgt", axis=1, tiled=True)
        projected = jnp.dot(
            mixed_full, gathered[3][layer_idx] * o_table, preferred_element_type=jnp.float32
        )
        post_squares = lax.psum(jnp.sum(projected * projected, axis=-1), "wgt")
        post = (
            projected
            * lax.rsqrt(post_squares / model_width + eps)[:, None]
            * post_gain[layer_idx][None, :]
        )
        state = (state.astype(jnp.float32) + post).astype(jnp.bfloat16)
    return state


def solution(mesh):
    placed = (
        P("seq", "wgt"),
        P(None, "seq", "wgt"),
        P(None, "seq", "wgt"),
        P(None, "seq", "wgt"),
        P(None, "seq", "wgt"),
        P(None, None, "wgt"),
        P(None, None, "wgt"),
        P(None, None, "wgt"),
        P(),
        P(),
        P(None, "wgt"),
        P(),
        P(),
        P(),
    )
    return jax.shard_map(
        per_device, mesh=mesh, in_specs=placed, out_specs=P("seq", "wgt"), check_vma=False
    )
```

profile of v0, /device:TPU:0, one launch (start us, length us, event | category | flops | bytes accessed | tf_op | source)
XLA Modules:
  0.0 766.7 jit_solution(2744792067710179786)
XLA Ops:
  7.3 0.7 all-gather.11.cloned.1.call-update
  12.9 3.6 fusion.40
  16.5 51.1 %all-gather.9.cloned.1.call-done = bf16[384,5376]{1,0:T(8,128)(2,1)} async-done(((bf16[384,2688]{1,0:T(8,128)(2,1)}), bf16[384,5376]{1,0:T(8,128)(2,1)}) %all-gather.9.cloned.1.call-update) | async-done | bytes 4128784 | tf_op jit(solution)/shard_map/all_gather | solution.py:85
  67.7 3.1 fusion.18
  70.7 90.0 %all-gather.11.cloned.1.call-done = bf16[2,5376,512]{2,1,0:T(8,128)(2,1)} async-done(((bf16[2,336,512]{2,1,0:T(8,128)(2,1)}), bf16[2,5376,512]{2,1,0:T(8,128)(2,1)}) %all-gather.11.cloned.1.call-update) | async-done | bytes 11010064 | tf_op jit(solution)/shard_map/all_gather | solution.py:79
  161.0 6.8 broadcast_in_dim.41
  167.8 5.5 fusion.49
  173.2 2.2 collective-permute-start
  175.4 3.5 collective-permute-start.1
  178.9 2.0 collective-permute-start.2
  180.9 86.7 %all-gather.13.cloned.1.call-done = bf16[2,5376,512]{2,1,0:T(8,128)(2,1)} async-done(((bf16[2,336,512]{2,1,0:T(8,128)(2,1)}), bf16[2,5376,512]{2,1,0:T(8,128)(2,1)}) %all-gather.13.cloned.1.call-update) | async-done | bytes 11010064 | tf_op jit(solution)/shard_map/all_gather | solution.py:78
  267.8 6.8 broadcast_in_dim.44
  274.8 6.8 broadcast_in_dim.101
  281.6 4.7 fusion.24
  286.4 8.2 %copy.42 = bf16[512,5376]{1,0:T(8,128)(2,1)} copy(bf16[512,5376]{0,1:T(8,128)(2,1)} %get-tuple-element.12) | data formatting | bytes 11010048 | tf_op jit(solution)/shard_map/dot_general | solution.py:98
  294.6 6.7 multiply_reduce_fusion.5
  301.6 0.8 maximum_convert_fusion
  302.3 3.0 collective-permute-start.3
  305.3 4.2 collective-permute-start.4
  309.5 2.2 collective-permute-start.5
  311.7 0.7 copy-done.6
  312.5 1.2 pad_maximum_fusion
  313.7 1.6 copy.41
  315.2 78.7 %all-gather.15.cloned.1.call-done = bf16[2,5376,1024]{2,1,0:T(8,128)(2,1)} async-done(((bf16[2,336,1024]{2,1,0:T(8,128)(2,1)}), bf16[2,5376,1024]{2,1,0:T(8,128)(2,1)}) %all-gather.15.cloned.1.call-update) | async-done | bytes 22020112 | tf_op jit(solution)/shard_map/all_gather | solution.py:77
  394.1 6.8 broadcast_in_dim.46
  401.0 6.8 broadcast_in_dim.103
  407.8 16.1 %fusion.4 = (bf16[1024,5376]{0,1:T(8,128)(2,1)}, bf16[1024,5376]{0,1:T(8,128)(2,1)}) fusion(bf16[672,8,8,128]{3,2,1,0:T(8,128)(2,1)S(1)} %bitcast.229, bf16[2,5376,1024]{2,1,0:T(8,128)(2,1)} %all-gather.15.cloned.1.call-done, bf16[672,8,8,128]{3,2,1,0:T(8,128)(2,1)S(1)} %bitcast.228), kind=kLoop, calls=%fused_computation.11 | loop fusion | flops 11010048 | bytes 66060288 | tf_op jit(solution)/shard_map/dot_general | solution.py:95
  423.9 14.4 %copy.45 = bf16[1024,5376]{1,0:T(8,128)(2,1)} copy(bf16[1024,5376]{0,1:T(8,128)(2,1)} %get-tuple-element.10) | data formatting | bytes 22020096 | tf_op jit(solution)/shard_map/dot_general | solution.py:95
  438.3 10.3 %multiply_reduce_fusion.3 = (f32[384,8]{0,1:T(8,128)S(1)}, f32[384,8,128]{0,2,1:T(8,128)S(1)}) fusion(bf16[8,128,5376]{2,1,0:T(8,128)(2,1)} %bitcast.235, f32[5376]{0:T(1024)S(1)} %get-tuple-element.6, f32[384]{0:T(512)S(1)} %add_rsqrt_fusion.7, bf16[384,5376]{1,0:T(8,128)(2,1)} %all-gather.9.cloned.1.call-done), kind=kOutput, calls=%fused_computation.85 | convolution fusion | flops 4236899328 | bytes 16747008 | tf_op jit(solution)/shard_map/dot_general | solution.py:95
  449.1 1.7 copy.20
  450.8 1.6 copy.21
  452.5 12.5 %fusion.102 = (f32[4,2,384]{2,1,0:T(2,128)S(1)}, f32[4,2,384,1536]{2,3,1,0:T(8,128)}) fusion(pred[384,1536]{0,1:T(8,128)(4,1)S(1)} %get-tuple-element.22, bf16[384,4,128]{0,2,1:T(8,128)(2,1)} %maximum_convert_fusion, bf16[384,4,128]{0,2,1:T(8,128)(2,1)} %bitcast.17, bf16[384,4,128]{0,2,1:T(8,128)(2,1)} %bitcast.16, bf16[384,4,128]{0,2,1:T(8,128)(2,1)} %bitcast.15, ...), kind=kOutput, calls=%fused_computation.180 | convolution fusion | flops 1229587968 | bytes 22622208 | tf_op jit(solution)/shard_map/sub | solution.py:129
  465.0 9.0 %fusion.48 = bf16[4,128,2,384]{3,1,2,0:T(8,128)(2,1)} fusion(bf16[1536,4,128,1]{0,2,3,1:T(8,128)(2,1)S(1)} %bitcast.252, f32[4,2,384,1536]{2,3,1,0:T(8,128)} %get-tuple-element.42, f32[4,2,384]{2,1,0:T(2,128)S(1)} %get-tuple-element.41), kind=kOutput, calls=%fused_computation.87 | convolution fusion | flops 1217789952 | bytes 21245952 | tf_op jit(solution)/shard_map/kgqs,skd->qkgd/dot_general | solution.py:131
  474.7 42.5 %all-gather.19.cloned.1.call-done = bf16[2,2048,2688]{2,1,0:T(8,128)(2,1)} async-done(((bf16[2,128,2688]{2,1,0:T(8,128)(2,1)}), bf16[2,2048,2688]{2,1,0:T(8,128)(2,1)}) %all-gather.19.cloned.1.call-update) | async-done | bytes 22020112 | tf_op jit(solution)/shard_map/all_gather | solution.py:80
  517.2 28.6 %all-gather.17.cloned.1.call-done = bf16[384,2048]{0,1:T(8,128)(2,1)} async-done(((bf16[384,1024]{0,1:T(8,128)(2,1)}), bf16[384,2048]{0,1:T(8,128)(2,1)}) %all-gather.17.cloned.1.call-update) | async-done | bytes 1572880 | tf_op jit(solution)/shard_map/all_gather | solution.py:135
  545.8 0.7 broadcast_in_dim.48
  546.5 11.7 %multiply_reduce_fusion.1 = (f32[384]{0:T(512)S(1)}, f32[384,2688]{1,0:T(8,128)}) fusion(bf16[384,2048]{0,1:T(8,128)(2,1)} %all-gather.17.cloned.1.call-done, bf16[2048,2688]{1,0:T(8,128)(2,1)S(1)} %bitcast.237, bf16[2,2048,2688]{2,1,0:T(8,128)(2,1)} %all-gather.19.cloned.1.call-done), kind=kOutput, calls=%fused_computation.66 | convolution fusion | flops 4235427328 | bytes 27723264 | tf_op jit(solution)/shard_map/dot_general | solution.py:136
  558.3 4.9 psum.14
  563.2 4.9 add_convert_fusion.1
  568.3 8.2 %copy.47 = bf16[512,5376]{1,0:T(8,128)(2,1)} copy(bf16[512,5376]{0,1:T(8,128)(2,1)} %get-tuple-element.11) | data formatting | bytes 11010048 | tf_op jit(solution)/shard_map/dot_general | solution.py:98
  576.5 14.1 %copy.50 = bf16[1024,5376]{1,0:T(8,128)(2,1)} copy(bf16[1024,5376]{0,1:T(8,128)(2,1)} %get-tuple-element.9) | data formatting | bytes 22020096 | tf_op jit(solution)/shard_map/dot_general | solution.py:95
  590.6 33.7 %all-gather.21.cloned.1.call-done = bf16[384,5376]{1,0:T(8,128)(2,1)} async-done(((bf16[384,2688]{1,0:T(8,128)(2,1)}), bf16[384,5376]{1,0:T(8,128)(2,1)}) %all-gather.21.cloned.1.call-update) | async-done | bytes 4128784 | tf_op jit(solution)/shard_map/all_gather | solution.py:85
  624.3 3.2 fusion.21
  627.7 5.3 multiply_reduce_fusion.4
  633.3 0.8 maximum_convert_fusion.1
  634.0 3.4 collective-permute-start.9
  637.4 4.5 collective-permute-start.10
  642.1 6.8 broadcast_in_dim.50
  648.9 6.0 fusion.50
  654.9 2.1 collective-permute-start.6
  657.1 4.1 collective-permute-start.7
  661.2 2.3 collective-permute-start.8
  663.5 5.9 multiply_reduce_fusion.2
  669.8 3.1 collective-permute-start.11
  673.7 1.6 copy.31
  675.3 1.3 pad_maximum_fusion.1
  676.7 1.8 copy.46
  678.5 12.3 %fusion.103 = (f32[4,2,384]{2,1,0:T(2,128)S(1)}, f32[4,2,384,1536]{2,3,1,0:T(8,128)}) fusion(pred[384,1536]{0,1:T(8,128)(4,1)} %get-tuple-element.21, bf16[384,4,128]{0,2,1:T(8,128)(2,1)} %maximum_convert_fusion.1, bf16[384,4,128]{0,2,1:T(8,128)(2,1)} %bitcast.50, bf16[384,4,128]{0,2,1:T(8,128)(2,1)} %bitcast.49, bf16[384,4,128]{0,2,1:T(8,128)(2,1)} %bitcast.48, ...), kind=kOutput, calls=%fused_computation.181 | convolution fusion | flops 1229587968 | bytes 22622208 | tf_op jit(solution)/shard_map/sub | solution.py:129
  690.8 8.7 %fusion.47 = bf16[4,128,2,384]{3,1,2,0:T(8,128)(2,1)} fusion(bf16[1536,4,128,1]{0,2,3,1:T(8,128)(2,1)S(1)} %bitcast.253, f32[4,2,384,1536]{2,3,1,0:T(8,128)} %get-tuple-element.50, f32[4,2,384]{2,1,0:T(2,128)S(1)} %get-tuple-element.49), kind=kOutput, calls=%fused_computation.86 | convolution fusion | flops 1217789952 | bytes 21245952 | tf_op jit(solution)/shard_map/kgqs,skd->qkgd/dot_general | solution.py:131
  699.9 31.6 %all-gather.23.cloned.1.call-done = bf16[384,2048]{0,1:T(8,128)(2,1)} async-done(((bf16[384,1024]{0,1:T(8,128)(2,1)}), bf16[384,2048]{0,1:T(8,128)(2,1)}) %all-gather.23.cloned.1.call-update) | async-done | bytes 1572880 | tf_op jit(solution)/shard_map/all_gather | solution.py:135
  731.5 4.7 broadcast_in_dim.104
  736.2 14.3 %multiply_reduce_fusion = (f32[384]{0:T(512)S(1)}, f32[384,2688]{1,0:T(8,128)}) fusion(bf16[384,2048]{0,1:T(8,128)(2,1)S(1)} %copy-done.21, bf16[2048,2688]{1,0:T(8,128)(2,1)} %bitcast.236, bf16[2,2048,2688]{2,1,0:T(8,128)(2,1)} %all-gather.19.cloned.1.call-done), kind=kOutput, calls=%fused_computation.64 | convolution fusion | flops 4235427328 | bytes 27723264 | tf_op jit(solution)/shard_map/dot_general | solution.py:136
  750.5 4.9 psum.15
  755.4 4.2 add_convert_fusion
  (126 shorter events, 10.0 us)
Async XLA Ops:
  6.5 3.5 copy-start.14
  6.5 3.7 copy-start.13
  6.5 4.0 copy-start.15
  6.5 4.1 copy-start.17
  6.5 4.7 copy-start.9
  6.5 4.8 copy-start.19
  6.6 5.4 copy-start.20
  6.6 61.1 %all-gather.9.cloned.1.call-start = ((), (), s32[]{:S(2)}) async-start(), calls=%async_computation | async-start | bytes 6193152 | tf_op jit(solution)/shard_map/all_gather | solution.py:85
  7.3 153.5 %all-gather.11.cloned.1.call-start = ((), (), s32[]{:S(2)}) async-start(), calls=%async_computation.1 | async-start | bytes 11698176 | tf_op jit(solution)/shard_map/all_gather | solution.py:79
  8.1 259.6 %all-gather.13.cloned.1.call-start = ((), (), s32[]{:S(2)}) async-start(), calls=%async_computation.2 | async-start | bytes 11698176 | tf_op jit(solution)/shard_map/all_gather | solution.py:78
  8.8 385.1 %all-gather.15.cloned.1.call-start = ((), (), s32[]{:S(2)}) async-start(), calls=%async_computation.3 | async-start | bytes 23396352 | tf_op jit(solution)/shard_map/all_gather | solution.py:77
  9.4 507.8 %all-gather.19.cloned.1.call-start = ((), (), s32[]{:S(2)}) async-start(), calls=%async_computation.5 | async-start | bytes 23396352 | tf_op jit(solution)/shard_map/all_gather | solution.py:80
  10.0 535.8 %all-gather.17.cloned.1.call-start = ((), (), s32[]{:S(2)}) async-start(), calls=%async_computation.4 | async-start | bytes 2359296 | tf_op jit(solution)/shard_map/all_gather | solution.py:135
  160.8 7.0 copy-start.2
  173.2 136.3 %collective-permute-start = (bf16[384,512]{1,0:T(8,128)(2,1)S(1)}, bf16[384,512]{1,0:T(8,128)(2,1)S(1)}, u32[]{:S(2)}, u32[]{:S(2)}) collective-permute-start(bf16[384,512]{1,0:T(8,128)(2,1)S(1)} %fusion.49), channel_id=1, source_target_pairs={{0,6},{2,8},{4,10},{6,12},{8,14},{10,16},{12,18},{14,20},{16,22},{... | collective-permute-start | bytes 1179656 | tf_op jit(solution)/shard_map/ppermute | solution.py:18
  175.4 136.3 %collective-permute-start.1 = (bf16[384,512]{1,0:T(8,128)(2,1)S(1)}, bf16[384,512]{1,0:T(8,128)(2,1)S(1)}, u32[]{:S(2)}, u32[]{:S(2)}) collective-permute-start(bf16[384,512]{1,0:T(8,128)(2,1)S(1)} %fusion.49), channel_id=1, source_target_pairs={{0,4},{2,6},{4,8},{6,10},{8,12},{10,14},{12,16},{14,18},{16,20},{1... | collective-permute-start | bytes 1179656 | tf_op jit(solution)/shard_map/ppermute | solution.py:18
  178.9 133.5 %collective-permute-start.2 = (bf16[384,512]{1,0:T(8,128)(2,1)S(1)}, bf16[384,512]{1,0:T(8,128)(2,1)}, u32[]{:S(2)}, u32[]{:S(2)}) collective-permute-start(bf16[384,512]{1,0:T(8,128)(2,1)S(1)} %fusion.49), channel_id=1, source_target_pairs={{0,2},{2,4},{4,6},{6,8},{8,10},{10,12},{12,14},{14,16},{16,18},{18... | collective-permute-start | bytes 1179656 | tf_op jit(solution)/shard_map/ppermute | solution.py:18
  267.8 13.8 %copy-start.1 = (bf16[2,5376,512]{2,1,0:T(8,128)(2,1)S(1)}, bf16[2,5376,512]{2,1,0:T(8,128)(2,1)}, u32[]{:S(2)}) copy-start(bf16[2,5376,512]{2,1,0:T(8,128)(2,1)} %all-gather.13.cloned.1.call-done) | copy-start | bytes 33030148
  302.3 150.1 %collective-permute-start.3 = (bf16[384,512]{0,1:T(8,128)(2,1)}, bf16[384,512]{0,1:T(8,128)(2,1)}, u32[]{:S(2)}, u32[]{:S(2)}) collective-permute-start(bf16[384,512]{0,1:T(8,128)(2,1)} %bitcast.14), channel_id=1, source_target_pairs={{0,6},{2,8},{4,10},{6,12},{8,14},{10,16},{12,18},{14,20},{16,22},{... | collective-permute-start | bytes 1179656 | tf_op jit(solution)/shard_map/ppermute | solution.py:18
  305.3 147.1 %collective-permute-start.4 = (bf16[384,512]{0,1:T(8,128)(2,1)}, bf16[384,512]{0,1:T(8,128)(2,1)}, u32[]{:S(2)}, u32[]{:S(2)}) collective-permute-start(bf16[384,512]{0,1:T(8,128)(2,1)} %bitcast.14), channel_id=1, source_target_pairs={{0,4},{2,6},{4,8},{6,10},{8,12},{10,14},{12,16},{14,18},{16,20},{1... | collective-permute-start | bytes 1179656 | tf_op jit(solution)/shard_map/ppermute | solution.py:18
  309.5 143.0 %collective-permute-start.5 = (bf16[384,512]{0,1:T(8,128)(2,1)}, bf16[384,512]{0,1:T(8,128)(2,1)}, u32[]{:S(2)}, u32[]{:S(2)}) collective-permute-start(bf16[384,512]{0,1:T(8,128)(2,1)} %bitcast.14), channel_id=1, source_target_pairs={{0,2},{2,4},{4,6},{6,8},{8,10},{10,12},{12,14},{14,16},{16,18},{18... | collective-permute-start | bytes 1179656 | tf_op jit(solution)/shard_map/ppermute | solution.py:18
  311.7 0.7 copy-start.6
  452.5 12.5 %copy-start.4 = (bf16[1536,512]{0,1:T(8,128)(2,1)S(1)}, bf16[1536,512]{0,1:T(8,128)(2,1)}, u32[]{:S(2)}) copy-start(bf16[1536,512]{0,1:T(8,128)(2,1)} %copy.41) | copy-start | bytes 4718596
  465.0 9.3 %copy-start.10 = (f32[2,2688]{1,0:T(2,128)S(1)}, f32[2,2688]{1,0:T(2,128)}, u32[]{:S(2)}) copy-start(f32[2,2688]{1,0:T(2,128)} %param.24) | copy-start | bytes 64516
  465.0 9.4 %copy-start.22 = (s32[2,16,42]{2,1,0:T(8,128)S(1)}, s32[2,16,42]{2,1,0:T(8,128)}, u32[]{:S(2)}) copy-start(s32[2,16,42]{2,1,0:T(8,128)} %param.22) | copy-start | bytes 16132
  474.0 150.3 %all-gather.21.cloned.1.call-start = ((), (), s32[]{:S(2)}) async-start(), calls=%async_computation.6 | async-start | bytes 6193152 | tf_op jit(solution)/shard_map/all_gather | solution.py:85
  474.3 72.2 %copy-start.11 = (s32[2688]{0:T(1024)}, s32[2688]{0:T(1024)S(1)}, u32[]{:S(2)}) copy-start(s32[2688]{0:T(1024)S(1)} %add_select_fusion) | copy-start | bytes 32260
  568.1 163.4 %all-gather.23.cloned.1.call-start = ((), (), s32[]{:S(2)}) async-start(), calls=%async_computation.7 | async-start | bytes 2359296 | tf_op jit(solution)/shard_map/all_gather | solution.py:135
  624.3 3.4 copy-start.3
  627.7 5.3 copy-start.16
  634.0 44.4 %collective-permute-start.9 = (bf16[384,512]{0,1:T(8,128)(2,1)}, bf16[384,512]{0,1:T(8,128)(2,1)}, u32[]{:S(2)}, u32[]{:S(2)}) collective-permute-start(bf16[384,512]{0,1:T(8,128)(2,1)} %bitcast.47), channel_id=1, source_target_pairs={{0,6},{2,8},{4,10},{6,12},{8,14},{10,16},{12,18},{14,20},{16,22},{... | collective-permute-start | bytes 1179656 | tf_op jit(solution)/shard_map/ppermute | solution.py:18
  637.4 41.0 %collective-permute-start.10 = (bf16[384,512]{0,1:T(8,128)(2,1)}, bf16[384,512]{0,1:T(8,128)(2,1)}, u32[]{:S(2)}, u32[]{:S(2)}) collective-permute-start(bf16[384,512]{0,1:T(8,128)(2,1)} %bitcast.47), channel_id=1, source_target_pairs={{0,4},{2,6},{4,8},{6,10},{8,12},{10,14},{12,16},{14,18},{16,20},{1... | collective-permute-start | bytes 1179656 | tf_op jit(solution)/shard_map/ppermute | solution.py:18
  642.1 21.4 %slice-start = ((s8[11010048]{0:T(1024)(128)(4,1)}), s8[4194304]{0:T(1024)(128)(4,1)S(1)}, s32[]{:S(2)}) async-start(s8[11010048]{0:T(1024)(128)(4,1)} %bitcast.232), calls=%async_computation.8 | async-start | bytes 8388608
  648.9 14.6 %slice-start.1 = ((s8[11010048]{0:T(1024)(128)(4,1)}), s8[4194304]{0:T(1024)(128)(4,1)S(1)}, s32[]{:S(2)}) async-start(s8[11010048]{0:T(1024)(128)(4,1)} %bitcast.232), calls=%async_computation.9 | async-start | bytes 8388608
  648.9 14.6 %slice-start.2 = ((s8[11010048]{0:T(1024)(128)(4,1)}), s8[2621440]{0:T(1024)(128)(4,1)S(1)}, s32[]{:S(2)}) async-start(s8[11010048]{0:T(1024)(128)(4,1)} %bitcast.232), calls=%async_computation.10 | async-start | bytes 5242880
  654.9 14.9 %collective-permute-start.6 = (bf16[384,512]{1,0:T(8,128)(2,1)}, bf16[384,512]{1,0:T(8,128)(2,1)S(1)}, u32[]{:S(2)}, u32[]{:S(2)}) collective-permute-start(bf16[384,512]{1,0:T(8,128)(2,1)} %fusion.50), channel_id=1, source_target_pairs={{0,6},{2,8},{4,10},{6,12},{8,14},{10,16},{12,18},{14,20},{16,22},{... | collective-permute-start | bytes 1179656 | tf_op jit(solution)/shard_map/ppermute | solution.py:18
  657.1 18.2 %collective-permute-start.7 = (bf16[384,512]{1,0:T(8,128)(2,1)}, bf16[384,512]{1,0:T(8,128)(2,1)}, u32[]{:S(2)}, u32[]{:S(2)}) collective-permute-start(bf16[384,512]{1,0:T(8,128)(2,1)} %fusion.50), channel_id=1, source_target_pairs={{0,4},{2,6},{4,8},{6,10},{8,12},{10,14},{12,16},{14,18},{16,20},{1... | collective-permute-start | bytes 1179656 | tf_op jit(solution)/shard_map/ppermute | solution.py:18
  661.2 14.1 %collective-permute-start.8 = (bf16[384,512]{1,0:T(8,128)(2,1)}, bf16[384,512]{1,0:T(8,128)(2,1)}, u32[]{:S(2)}, u32[]{:S(2)}) collective-permute-start(bf16[384,512]{1,0:T(8,128)(2,1)} %fusion.50), channel_id=1, source_target_pairs={{0,2},{2,4},{4,6},{6,8},{8,10},{10,12},{12,14},{14,16},{16,18},{18... | collective-permute-start | bytes 1179656 | tf_op jit(solution)/shard_map/ppermute | solution.py:18
  663.5 6.0 copy-start.18
  669.8 3.3 copy-start.7
  669.8 8.6 %collective-permute-start.11 = (bf16[384,512]{0,1:T(8,128)(2,1)}, bf16[384,512]{0,1:T(8,128)(2,1)}, u32[]{:S(2)}, u32[]{:S(2)}) collective-permute-start(bf16[384,512]{0,1:T(8,128)(2,1)} %bitcast.47), channel_id=1, source_target_pairs={{0,2},{2,4},{4,6},{6,8},{8,10},{10,12},{12,14},{14,16},{16,18},{18... | collective-permute-start | bytes 1179656 | tf_op jit(solution)/shard_map/ppermute | solution.py:18
  673.2 2.1 copy-start.8
  678.4 12.3 %copy-start.5 = (bf16[1536,512]{0,1:T(8,128)(2,1)S(1)}, bf16[1536,512]{0,1:T(8,128)(2,1)}, u32[]{:S(2)}) copy-start(bf16[1536,512]{0,1:T(8,128)(2,1)} %copy.46) | copy-start | bytes 4718596
  690.8 8.8 %copy-start.12 = (s32[2688]{0:T(1024)S(1)}, s32[2688]{0:T(1024)}, u32[]{:S(2)}) copy-start(s32[2688]{0:T(1024)} %copy-done.11) | copy-start | bytes 32260
  690.8 8.8 %copy-start.23 = (s32[2,16,42]{2,1,0:T(8,128)S(1)}, s32[2,16,42]{2,1,0:T(8,128)}, u32[]{:S(2)}) copy-start(s32[2,16,42]{2,1,0:T(8,128)} %param.22) | copy-start | bytes 16132
  731.5 4.7 copy-start.21
  736.2 19.2 %copy-start = (bf16[384,2688]{1,0:T(8,128)(2,1)S(1)}, bf16[384,2688]{1,0:T(8,128)(2,1)}, u32[]{:S(2)}) copy-start(bf16[384,2688]{1,0:T(8,128)(2,1)} %add_convert_fusion.1) | copy-start | bytes 6193156
Sparse Core Ops, SparseCore 0:
  8.9 58.6 all-gather.8
  69.9 90.7 all-gather.10
  163.1 104.5 all-gather.12
  269.0 124.8 all-gather.14
  395.3 121.8 all-gather.18
  518.6 27.1 all-gather.16
  568.2 55.9 all-gather.20
  699.7 31.7 all-gather.22
where the time goes:
time: 775 us; the launch traced here: 767 us
  waiting for transfers between devices  446 us (58%)
  matrix products  109 us (14%)
  local copies, waits for them, and re-layouts  105 us (14%)
  other arithmetic  46 us (6%)
  starting transfers between devices  37.1 us (5%)
  between operations  14.4 us (2%)
  blocking collectives  9.82 us (1%)
    all_gather x1, waiting for transfers between devices, per_device(): lax.all_gather(v_weight, 'seq', axis=1, tiled=True)  90 us
    all_gather x1, waiting for transfers between devices, per_device(): lax.all_gather(k_weight, 'seq', axis=1, tiled=True)  86.7 us
    all_gather x2, waiting for transfers between devices, per_device(): arriving = lax.all_gather(outgoing, 'wgt', axis=1, tiled=True)  84.8 us
    all_gather x1, waiting for transfers between devices, per_device(): lax.all_gather(q_weight, 'seq', axis=1, tiled=True)  78.7 us
    all_gather x2, waiting for transfers between devices, per_device(): mixed_full = lax.all_gather(mixed, 'wgt', axis=1, tiled=True)  60.2 us
    all_gather x1, waiting for transfers between devices, per_device(): lax.all_gather(o_weight, 'seq', axis=1, tiled=True)  42.5 us
    broadcast_in_dim x6, local copies, waits for them, and re-layouts, expand_scales(): jnp.repeat(jnp.repeat(factor, BLOCK, axis=0), BLOCK, axis=1)  40.7 us
    ppermute x12, starting transfers between devices, passed_along(): return lax.ppermute(array, axis, pairs)  36.6 us
  transfers between devices with their start and end apart: 20, of which 8 were waited for; matrix products, arithmetic and copies ran while one was open for 24% of the time, Pallas kernels for 0%

commit v1 on v0

--- a/solution.py
+++ b/solution.py
@@ -82,7 +82,7 @@
     state = hidden
     for layer_idx in range(LAYERS):
         outgoing = state
-        arriving = lax.all_gather(outgoing, "wgt", axis=1, tiled=True)
+        arriving = jnp.concatenate(lax.all_gather(outgoing, "wgt"), axis=1)
         normed = rmsnorm(arriving.astype(jnp.float32), in_gain[layer_idx]).astype(jnp.bfloat16)
         tables = (
             expand_scales(q_scale[layer_idx]),

time: 775 us -> 799 us (1.031)
  local copies, waits for them, and re-layouts: 105 us -> 182 us
  waiting for transfers between devices: 446 us -> 380 us
    convert_element_type x0 -> x8, local copies, waits for them, and re-layouts: none -> 57.5 us  [the longest x6 37.2 us: per_device(): rmsnorm(arriving.astype(jnp.float32), in_gain[layer_idx])]
    all_gather x2, waiting for transfers between devices: 84.8 us -> 31.4 us  [per_device(): arriving = jnp.concatenate(lax.all_gather(outgoing, 'wgt'), axis=1)]
    all_gather x1, waiting for transfers between devices: 90 us -> 65.6 us  [per_device(): lax.all_gather(v_weight, 'seq', axis=1, tiled=True)]
    broadcast_in_dim x6, local copies, waits for them, and re-layouts: 40.7 us -> 59.3 us  [expand_scales(): jnp.repeat(jnp.repeat(factor, BLOCK, axis=0), BLOCK, axis=1)]
  transfers between devices with their start and end apart: 20 -> 20, of which waited for: 8 -> 8; matrix products, arithmetic and copies ran while one was open for 24% -> 32% of each run, Pallas kernels for 0% -> 0%
where the time goes in v1:
time: 799 us; the launch traced here: 788 us
  waiting for transfers between devices  380 us (48%)
  local copies, waits for them, and re-layouts  182 us (23%)
  matrix products  112 us (14%)
  other arithmetic  52.7 us (7%)
  starting transfers between devices  37.3 us (5%)
  between operations  14.6 us (2%)
  blocking collectives  9.82 us (1%)
    all_gather x1, waiting for transfers between devices, per_device(): lax.all_gather(k_weight, 'seq', axis=1, tiled=True)  93.5 us
    all_gather x1, waiting for transfers between devices, per_device(): lax.all_gather(q_weight, 'seq', axis=1, tiled=True)  78.8 us
    all_gather x1, waiting for transfers between devices, per_device(): lax.all_gather(v_weight, 'seq', axis=1, tiled=True)  65.6 us
    all_gather x2, waiting for transfers between devices, per_device(): mixed_full = lax.all_gather(mixed, 'wgt', axis=1, tiled=True)  65.4 us
    broadcast_in_dim x6, local copies, waits for them, and re-layouts, expand_scales(): jnp.repeat(jnp.repeat(factor, BLOCK, axis=0), BLOCK, axis=1)  59.3 us
    all_gather x1, waiting for transfers between devices, per_device(): lax.all_gather(o_weight, 'seq', axis=1, tiled=True)  42.2 us
    convert_element_type x6, local copies, waits for them, and re-layouts, per_device(): rmsnorm(arriving.astype(jnp.float32), in_gain[layer_idx])  37.2 us
    ppermute x12, starting transfers between devices, passed_along(): return lax.ppermute(array, axis, pairs)  36.4 us
  transfers between devices with their start and end apart: 20, of which 8 were waited for; matrix products, arithmetic and copies ran while one was open for 32% of the time, Pallas kernels for 0%

profile of v1, /device:TPU:0, one launch (start us, length us, event | category | flops | bytes accessed | tf_op | source)
XLA Modules:
  0.0 788.0 jit_solution(11724956123383834794)
XLA Ops:
  10.9 16.1 %broadcast_in_dim.41 = bf16[5376,4,128]{2,1,0:T(4,128)(2,1)} broadcast(bf16[5376,4]{1,0:T(8,128)(2,1)S(1)} %bitcast.234), dimensions={0,1} | broadcast | bytes 5548032 | tf_op jit(solution)/shard_map/broadcast_in_dim | solution.py:40
  27.0 10.2 %convert_element_type.236 = bf16[1,5376,512]{2,1,0:T(8,128)(2,1)} reshape(bf16[5376,4,128]{2,1,0:T(4,128)(2,1)} %broadcast_in_dim.41) | data formatting | bytes 11010048 | tf_op jit(solution)/shard_map/convert_element_type | solution.py:40
  39.3 3.5 fusion.34
  42.9 24.8 %all-gather.23.cloned.1.call-done = bf16[768,2688]{1,0:T(8,128)(2,1)} async-done(((bf16[384,2688]{1,0:T(8,128)(2,1)}), bf16[768,2688]{1,0:T(8,128)(2,1)}) %all-gather.23.cloned.1.call-update) | async-done | bytes 4128784 | tf_op jit(solution)/shard_map/all_gather | solution.py:85
  67.6 3.2 fusion.18
  71.0 3.2 fusion.52
  74.3 6.3 copy.15
  80.6 10.0 %reshape.365 = bf16[384,5376,1]{1,0,2:T(8,128)(2,1)} reshape(bf16[384,2,2688]{2,1,0:T(2,128)(2,1)} %copy.15) | data formatting | bytes 8257536 | tf_op jit(solution)/shard_map/convert_element_type | solution.py:86
  90.6 4.6 copy.53
  95.1 65.6 %all-gather.11.cloned.1.call-done = bf16[2,5376,512]{2,1,0:T(8,128)(2,1)} async-done(((bf16[2,336,512]{2,1,0:T(8,128)(2,1)}), bf16[2,5376,512]{2,1,0:T(8,128)(2,1)}) %all-gather.11.cloned.1.call-update) | async-done | bytes 11010064 | tf_op jit(solution)/shard_map/all_gather | solution.py:79
  160.7 7.7 fusion.43
  168.4 2.3 collective-permute-start
  170.8 3.5 collective-permute-start.1
  174.2 2.1 collective-permute-start.2
  176.3 93.5 %all-gather.13.cloned.1.call-done = bf16[2,5376,512]{2,1,0:T(8,128)(2,1)} async-done(((bf16[2,336,512]{2,1,0:T(8,128)(2,1)}), bf16[2,5376,512]{2,1,0:T(8,128)(2,1)}) %all-gather.13.cloned.1.call-update) | async-done | bytes 11010064 | tf_op jit(solution)/shard_map/all_gather | solution.py:78
  270.0 6.8 broadcast_in_dim.44
  277.0 6.8 broadcast_in_dim.101
  283.8 4.7 fusion.24
  288.5 8.4 %copy.44 = bf16[512,5376]{1,0:T(8,128)(2,1)} copy(bf16[512,5376]{0,1:T(8,128)(2,1)} %get-tuple-element.12) | data formatting | bytes 11010048 | tf_op jit(solution)/shard_map/dot_general | solution.py:98
  296.9 6.5 multiply_reduce_fusion.5
  304.4 3.0 collective-permute-start.3
  307.4 4.2 collective-permute-start.4
  311.7 2.0 collective-permute-start.5
  317.3 78.8 %all-gather.15.cloned.1.call-done = bf16[2,5376,1024]{2,1,0:T(8,128)(2,1)} async-done(((bf16[2,336,1024]{2,1,0:T(8,128)(2,1)}), bf16[2,5376,1024]{2,1,0:T(8,128)(2,1)}) %all-gather.15.cloned.1.call-update) | async-done | bytes 22020112 | tf_op jit(solution)/shard_map/all_gather | solution.py:77
  396.3 6.8 broadcast_in_dim.46
  403.2 6.8 broadcast_in_dim.103
  410.0 16.1 %fusion.4 = (bf16[1024,5376]{0,1:T(8,128)(2,1)}, bf16[1024,5376]{0,1:T(8,128)(2,1)}) fusion(bf16[672,8,8,128]{3,2,1,0:T(8,128)(2,1)S(1)} %bitcast.215, bf16[2,5376,1024]{2,1,0:T(8,128)(2,1)} %all-gather.15.cloned.1.call-done, bf16[672,8,8,128]{3,2,1,0:T(8,128)(2,1)S(1)} %bitcast.214), kind=kLoop, calls=%fused_computation.11 | loop fusion | flops 11010048 | bytes 66060288 | tf_op jit(solution)/shard_map/dot_general | solution.py:95
  426.1 14.8 %copy.47 = bf16[1024,5376]{1,0:T(8,128)(2,1)} copy(bf16[1024,5376]{0,1:T(8,128)(2,1)} %get-tuple-element.10) | data formatting | bytes 22020096 | tf_op jit(solution)/shard_map/dot_general | solution.py:95
  441.0 10.0 %multiply_reduce_fusion.3 = (f32[384,8]{0,1:T(8,128)S(1)}, f32[384,8,128]{0,2,1:T(8,128)S(1)}) fusion(bf16[384,5376,1]{1,0,2:T(8,128)(2,1)} %reshape.365, bf16[8,128,5376]{2,1,0:T(8,128)(2,1)} %bitcast.226), kind=kOutput, calls=%fused_computation.75 | convolution fusion | flops 4228641792 | bytes 16723968 | tf_op jit(solution)/shard_map/dot_general | solution.py:95
  451.5 1.7 copy.21
  454.8 12.5 %fusion.98 = (f32[4,2,384]{2,1,0:T(2,128)S(1)}, f32[4,2,384,1536]{2,3,1,0:T(8,128)}) fusion(pred[384,1536]{0,1:T(8,128)(4,1)S(1)} %get-tuple-element.26, bf16[384,4,128]{0,2,1:T(8,128)(2,1)} %maximum_convert_fusion, bf16[384,4,128]{0,2,1:T(8,128)(2,1)} %bitcast.19, bf16[384,4,128]{0,2,1:T(8,128)(2,1)} %bitcast.18, bf16[384,4,128]{0,2,1:T(8,128)(2,1)} %bitcast.17, ...), kind=kOutput, calls=%fused_computation.174 | convolution fusion | flops 1229587968 | bytes 22622208 | tf_op jit(solution)/shard_map/sub | solution.py:129
  467.3 9.0 %fusion.42 = bf16[4,128,2,384]{3,1,2,0:T(8,128)(2,1)} fusion(bf16[1536,4,128,1]{0,2,3,1:T(8,128)(2,1)S(1)} %bitcast.244, f32[4,2,384,1536]{2,3,1,0:T(8,128)} %get-tuple-element.46, f32[4,2,384]{2,1,0:T(2,128)S(1)} %get-tuple-element.45), kind=kOutput, calls=%fused_computation.77 | convolution fusion | flops 1217789952 | bytes 21245952 | tf_op jit(solution)/shard_map/kgqs,skd->qkgd/dot_general | solution.py:131
  477.2 42.2 %all-gather.19.cloned.1.call-done = bf16[2,2048,2688]{2,1,0:T(8,128)(2,1)} async-done(((bf16[2,128,2688]{2,1,0:T(8,128)(2,1)}), bf16[2,2048,2688]{2,1,0:T(8,128)(2,1)}) %all-gather.19.cloned.1.call-update) | async-done | bytes 22020112 | tf_op jit(solution)/shard_map/all_gather | solution.py:80
  519.4 28.6 %all-gather.17.cloned.1.call-done = bf16[384,2048]{0,1:T(8,128)(2,1)} async-done(((bf16[384,1024]{0,1:T(8,128)(2,1)}), bf16[384,2048]{0,1:T(8,128)(2,1)}) %all-gather.17.cloned.1.call-update) | async-done | bytes 1572880 | tf_op jit(solution)/shard_map/all_gather | solution.py:135
  548.7 11.7 %multiply_reduce_fusion.1 = (f32[384]{0:T(512)S(1)}, f32[384,2688]{1,0:T(8,128)}) fusion(bf16[384,2048]{0,1:T(8,128)(2,1)} %all-gather.17.cloned.1.call-done, bf16[2048,2688]{1,0:T(8,128)(2,1)S(1)} %bitcast.227, bf16[2,2048,2688]{2,1,0:T(8,128)(2,1)} %all-gather.19.cloned.1.call-done), kind=kOutput, calls=%fused_computation.56 | convolution fusion | flops 4235427328 | bytes 27723264 | tf_op jit(solution)/shard_map/dot_general | solution.py:136
  560.4 4.9 psum.14
  565.3 4.9 add_convert_fusion.1
  570.8 16.1 %broadcast_in_dim.50 = bf16[5376,4,128]{2,1,0:T(4,128)(2,1)} broadcast(bf16[5376,4]{1,0:T(8,128)(2,1)S(1)} %bitcast.237), dimensions={0,1} | broadcast | bytes 5548032 | tf_op jit(solution)/shard_map/broadcast_in_dim | solution.py:40
  586.9 10.1 %convert_element_type.263 = bf16[1,5376,512]{2,1,0:T(8,128)(2,1)} reshape(bf16[5376,4,128]{2,1,0:T(4,128)(2,1)} %broadcast_in_dim.50) | data formatting | bytes 11010048 | tf_op jit(solution)/shard_map/convert_element_type | solution.py:40
  597.0 8.0 %copy.49 = bf16[512,5376]{1,0:T(8,128)(2,1)} copy(bf16[512,5376]{0,1:T(8,128)(2,1)} %get-tuple-element.11) | data formatting | bytes 11010048 | tf_op jit(solution)/shard_map/dot_general | solution.py:98
  605.0 14.7 %copy.52 = bf16[1024,5376]{1,0:T(8,128)(2,1)} copy(bf16[1024,5376]{0,1:T(8,128)(2,1)} %get-tuple-element.9) | data formatting | bytes 22020096 | tf_op jit(solution)/shard_map/dot_general | solution.py:95
  619.7 6.7 all-gather.25.cloned.1.call-done
  626.4 3.2 fusion.21
  629.8 3.3 fusion.50
  633.1 6.2 copy.26
  639.3 9.9 %reshape.368 = bf16[384,5376,1]{1,0,2:T(8,128)(2,1)} reshape(bf16[384,2,2688]{2,1,0:T(2,128)(2,1)} %copy.26) | data formatting | bytes 8257536 | tf_op jit(solution)/shard_map/convert_element_type | solution.py:86
  649.2 6.6 multiply_reduce_fusion.4
  656.9 3.4 collective-permute-start.9
  660.3 4.1 collective-permute-start.10
  664.8 5.9 fusion.46
  670.7 2.1 collective-permute-start.6
  672.9 4.1 collective-permute-start.7
  677.0 2.3 collective-permute-start.8
  679.4 5.9 multiply_reduce_fusion.2
  685.6 3.1 collective-permute-start.11
  689.4 1.6 copy.33
  692.4 1.8 copy.48
  694.3 12.3 %fusion.99 = (f32[4,2,384]{2,1,0:T(2,128)S(1)}, f32[4,2,384,1536]{2,3,1,0:T(8,128)}) fusion(pred[384,1536]{0,1:T(8,128)(4,1)} %get-tuple-element.25, bf16[384,4,128]{0,2,1:T(8,128)(2,1)} %maximum_convert_fusion.1, bf16[384,4,128]{0,2,1:T(8,128)(2,1)} %bitcast.54, bf16[384,4,128]{0,2,1:T(8,128)(2,1)} %bitcast.53, bf16[384,4,128]{0,2,1:T(8,128)(2,1)} %bitcast.52, ...), kind=kOutput, calls=%fused_computation.175 | convolution fusion | flops 1229587968 | bytes 22622208 | tf_op jit(solution)/shard_map/sub | solution.py:129
  706.6 8.7 %fusion.41 = bf16[4,128,2,384]{3,1,2,0:T(8,128)(2,1)} fusion(bf16[1536,4,128,1]{0,2,3,1:T(8,128)(2,1)S(1)} %bitcast.245, f32[4,2,384,1536]{2,3,1,0:T(8,128)} %get-tuple-element.54, f32[4,2,384]{2,1,0:T(2,128)S(1)} %get-tuple-element.53), kind=kOutput, calls=%fused_computation.76 | convolution fusion | flops 1217789952 | bytes 21245952 | tf_op jit(solution)/shard_map/kgqs,skd->qkgd/dot_general | solution.py:131
  715.6 36.8 %all-gather.21.cloned.1.call-done = bf16[384,2048]{0,1:T(8,128)(2,1)} async-done(((bf16[384,1024]{0,1:T(8,128)(2,1)}), bf16[384,2048]{0,1:T(8,128)(2,1)}) %all-gather.21.cloned.1.call-update) | async-done | bytes 1572880 | tf_op jit(solution)/shard_map/all_gather | solution.py:135
  752.5 4.8 broadcast_in_dim.104
  757.2 14.3 %multiply_reduce_fusion = (f32[384]{0:T(512)S(1)}, f32[384,2688]{1,0:T(8,128)}) fusion(bf16[384,2048]{0,1:T(8,128)(2,1)S(1)} %copy-done.23, bf16[2048,2688]{1,0:T(8,128)(2,1)} %bitcast.225, bf16[2,2048,2688]{2,1,0:T(8,128)(2,1)} %all-gather.19.cloned.1.call-done), kind=kOutput, calls=%fused_computation.54 | convolution fusion | flops 4235427328 | bytes 27723264 | tf_op jit(solution)/shard_map/dot_general | solution.py:136
  771.5 4.9 psum.15
  776.5 4.2 add_convert_fusion
  (147 shorter events, 20.5 us)
Async XLA Ops:
  6.5 3.4 copy-start.11
  6.5 3.6 copy-start.16
  6.5 3.8 copy-start.15
  6.5 4.1 copy-start.17
  6.5 61.1 %all-gather.23.cloned.1.call-start = ((), (), s32[]{:S(2)}) async-start(), calls=%async_computation.6 | async-start | bytes 6193152 | tf_op jit(solution)/shard_map/all_gather | solution.py:85
  7.3 153.5 %all-gather.11.cloned.1.call-start = ((), (), s32[]{:S(2)}) async-start(), calls=%async_computation | async-start | bytes 11698176 | tf_op jit(solution)/shard_map/all_gather | solution.py:79
  8.0 261.8 %all-gather.13.cloned.1.call-start = ((), (), s32[]{:S(2)}) async-start(), calls=%async_computation.1 | async-start | bytes 11698176 | tf_op jit(solution)/shard_map/all_gather | solution.py:78
  8.8 387.3 %all-gather.15.cloned.1.call-start = ((), (), s32[]{:S(2)}) async-start(), calls=%async_computation.2 | async-start | bytes 23396352 | tf_op jit(solution)/shard_map/all_gather | solution.py:77
  9.3 510.0 %all-gather.19.cloned.1.call-start = ((), (), s32[]{:S(2)}) async-start(), calls=%async_computation.4 | async-start | bytes 23396352 | tf_op jit(solution)/shard_map/all_gather | solution.py:80
  9.9 538.0 %all-gather.17.cloned.1.call-start = ((), (), s32[]{:S(2)}) async-start(), calls=%async_computation.3 | async-start | bytes 2359296 | tf_op jit(solution)/shard_map/all_gather | solution.py:135
  27.0 10.2 %copy-start.19 = (s32[2]{0:T(128)S(1)}, s32[2]{0:T(128)}, u32[]{:S(2)}) copy-start(s32[2]{0:T(128)} %param.27) | copy-start | bytes 28
  27.0 10.8 %copy-start.21 = (f32[2,128]{1,0:T(2,128)S(1)}, f32[2,128]{1,0:T(2,128)}, u32[]{:S(2)}) copy-start(f32[2,128]{1,0:T(2,128)} %param.26) | copy-start | bytes 3076
  27.0 11.3 %copy-start.22 = (f32[2,128]{1,0:T(2,128)S(1)}, f32[2,128]{1,0:T(2,128)}, u32[]{:S(2)}) copy-start(f32[2,128]{1,0:T(2,128)} %param.25) | copy-start | bytes 3076
  67.6 3.4 copy-start.1
  168.4 143.3 %collective-permute-start = (bf16[384,512]{1,0:T(8,128)(2,1)S(1)}, bf16[384,512]{1,0:T(8,128)(2,1)S(1)}, u32[]{:S(2)}, u32[]{:S(2)}) collective-permute-start(bf16[384,512]{1,0:T(8,128)(2,1)S(1)} %fusion.43), channel_id=1, source_target_pairs={{0,6},{2,8},{4,10},{6,12},{8,14},{10,16},{12,18},{14,20},{16,22},{... | collective-permute-start | bytes 1179656 | tf_op jit(solution)/shard_map/ppermute | solution.py:18
  170.8 143.0 %collective-permute-start.1 = (bf16[384,512]{1,0:T(8,128)(2,1)S(1)}, bf16[384,512]{1,0:T(8,128)(2,1)S(1)}, u32[]{:S(2)}, u32[]{:S(2)}) collective-permute-start(bf16[384,512]{1,0:T(8,128)(2,1)S(1)} %fusion.43), channel_id=1, source_target_pairs={{0,4},{2,6},{4,8},{6,10},{8,12},{10,14},{12,16},{14,18},{16,20},{1... | collective-permute-start | bytes 1179656 | tf_op jit(solution)/shard_map/ppermute | solution.py:18
  174.2 140.3 %collective-permute-start.2 = (bf16[384,512]{1,0:T(8,128)(2,1)S(1)}, bf16[384,512]{1,0:T(8,128)(2,1)}, u32[]{:S(2)}, u32[]{:S(2)}) collective-permute-start(bf16[384,512]{1,0:T(8,128)(2,1)S(1)} %fusion.43), channel_id=1, source_target_pairs={{0,2},{2,4},{4,6},{6,8},{8,10},{10,12},{12,14},{14,16},{16,18},{18... | collective-permute-start | bytes 1179656 | tf_op jit(solution)/shard_map/ppermute | solution.py:18
  270.0 13.8 %copy-start.4 = (bf16[2,5376,512]{2,1,0:T(8,128)(2,1)S(1)}, bf16[2,5376,512]{2,1,0:T(8,128)(2,1)}, u32[]{:S(2)}) copy-start(bf16[2,5376,512]{2,1,0:T(8,128)(2,1)} %all-gather.13.cloned.1.call-done) | copy-start | bytes 33030148
  304.4 150.4 %collective-permute-start.3 = (bf16[384,512]{0,1:T(8,128)(2,1)}, bf16[384,512]{0,1:T(8,128)(2,1)}, u32[]{:S(2)}, u32[]{:S(2)}) collective-permute-start(bf16[384,512]{0,1:T(8,128)(2,1)} %bitcast.16), channel_id=1, source_target_pairs={{0,6},{2,8},{4,10},{6,12},{8,14},{10,16},{12,18},{14,20},{16,22},{... | collective-permute-start | bytes 1179656 | tf_op jit(solution)/shard_map/ppermute | solution.py:18
  307.4 147.4 %collective-permute-start.4 = (bf16[384,512]{0,1:T(8,128)(2,1)}, bf16[384,512]{0,1:T(8,128)(2,1)}, u32[]{:S(2)}, u32[]{:S(2)}) collective-permute-start(bf16[384,512]{0,1:T(8,128)(2,1)} %bitcast.16), channel_id=1, source_target_pairs={{0,4},{2,6},{4,8},{6,10},{8,12},{10,14},{12,16},{14,18},{16,20},{1... | collective-permute-start | bytes 1179656 | tf_op jit(solution)/shard_map/ppermute | solution.py:18
  311.7 143.1 %collective-permute-start.5 = (bf16[384,512]{0,1:T(8,128)(2,1)}, bf16[384,512]{0,1:T(8,128)(2,1)}, u32[]{:S(2)}, u32[]{:S(2)}) collective-permute-start(bf16[384,512]{0,1:T(8,128)(2,1)} %bitcast.16), channel_id=1, source_target_pairs={{0,2},{2,4},{4,6},{6,8},{8,10},{10,12},{12,14},{14,16},{16,18},{18... | collective-permute-start | bytes 1179656 | tf_op jit(solution)/shard_map/ppermute | solution.py:18
  313.7 0.7 copy-start.8
  454.8 12.5 %copy-start.6 = (bf16[1536,512]{0,1:T(8,128)(2,1)S(1)}, bf16[1536,512]{0,1:T(8,128)(2,1)}, u32[]{:S(2)}) copy-start(bf16[1536,512]{0,1:T(8,128)(2,1)} %copy.43) | copy-start | bytes 4718596
  467.3 9.5 %copy-start.12 = (f32[2,2688]{1,0:T(2,128)S(1)}, f32[2,2688]{1,0:T(2,128)}, u32[]{:S(2)}) copy-start(f32[2,2688]{1,0:T(2,128)} %param.24) | copy-start | bytes 64516
  467.3 9.6 %copy-start.24 = (s32[2,16,42]{2,1,0:T(8,128)S(1)}, s32[2,16,42]{2,1,0:T(8,128)}, u32[]{:S(2)}) copy-start(s32[2,16,42]{2,1,0:T(8,128)} %param.22) | copy-start | bytes 16132
  476.3 150.1 %all-gather.25.cloned.1.call-start = ((), (), s32[]{:S(2)}) async-start(), calls=%async_computation.7 | async-start | bytes 6193152 | tf_op jit(solution)/shard_map/all_gather | solution.py:85
  476.8 71.9 %copy-start.13 = (s32[2688]{0:T(1024)}, s32[2688]{0:T(1024)S(1)}, u32[]{:S(2)}) copy-start(s32[2688]{0:T(1024)S(1)} %add_select_fusion) | copy-start | bytes 32260
  570.3 182.2 %all-gather.21.cloned.1.call-start = ((), (), s32[]{:S(2)}) async-start(), calls=%async_computation.5 | async-start | bytes 2359296 | tf_op jit(solution)/shard_map/all_gather | solution.py:135
  626.4 3.4 copy-start.2
  639.3 25.4 %slice-start.3 = ((s8[5505024]{0:T(1024)(128)(4,1)}), s8[1310720]{0:T(1024)(128)(4,1)S(1)}, s32[]{:S(2)}) async-start(s8[5505024]{0:T(1024)(128)(4,1)} %bitcast.230), calls=%async_computation.11 | async-start | bytes 2621440
  649.2 6.7 copy-start.18
  649.2 15.3 %copy-start.3 = (bf16[2,48,8,2688]{3,2,1,0:T(8,128)(2,1)S(1)}, bf16[2,48,8,2688]{3,2,1,0:T(8,128)(2,1)}, u32[]{:S(2)}) copy-start(bf16[2,48,8,2688]{3,2,1,0:T(8,128)(2,1)} %get-tuple-element.14) | copy-start | bytes 12386308
  649.2 15.6 %slice-start.4 = ((s8[5505024]{0:T(1024)(128)(4,1)}), s8[4194304]{0:T(1024)(128)(4,1)S(1)}, s32[]{:S(2)}) async-start(s8[5505024]{0:T(1024)(128)(4,1)} %bitcast.230), calls=%async_computation.12 | async-start | bytes 8388608
  656.9 37.3 %collective-permute-start.9 = (bf16[384,512]{0,1:T(8,128)(2,1)}, bf16[384,512]{0,1:T(8,128)(2,1)}, u32[]{:S(2)}, u32[]{:S(2)}) collective-permute-start(bf16[384,512]{0,1:T(8,128)(2,1)} %bitcast.51), channel_id=1, source_target_pairs={{0,6},{2,8},{4,10},{6,12},{8,14},{10,16},{12,18},{14,20},{16,22},{... | collective-permute-start | bytes 1179656 | tf_op jit(solution)/shard_map/ppermute | solution.py:18
  660.3 33.9 %collective-permute-start.10 = (bf16[384,512]{0,1:T(8,128)(2,1)}, bf16[384,512]{0,1:T(8,128)(2,1)}, u32[]{:S(2)}, u32[]{:S(2)}) collective-permute-start(bf16[384,512]{0,1:T(8,128)(2,1)} %bitcast.51), channel_id=1, source_target_pairs={{0,4},{2,6},{4,8},{6,10},{8,12},{10,14},{12,16},{14,18},{16,20},{1... | collective-permute-start | bytes 1179656 | tf_op jit(solution)/shard_map/ppermute | solution.py:18
  664.4 14.9 %slice-start = ((s8[11010048]{0:T(1024)(128)(4,1)}), s8[2621440]{0:T(1024)(128)(4,1)S(1)}, s32[]{:S(2)}) async-start(s8[11010048]{0:T(1024)(128)(4,1)} %bitcast.222), calls=%async_computation.8 | async-start | bytes 5242880
  664.8 14.6 %slice-start.1 = ((s8[11010048]{0:T(1024)(128)(4,1)}), s8[4194304]{0:T(1024)(128)(4,1)S(1)}, s32[]{:S(2)}) async-start(s8[11010048]{0:T(1024)(128)(4,1)} %bitcast.222), calls=%async_computation.9 | async-start | bytes 8388608
  664.8 14.6 %slice-start.2 = ((s8[11010048]{0:T(1024)(128)(4,1)}), s8[4194304]{0:T(1024)(128)(4,1)S(1)}, s32[]{:S(2)}) async-start(s8[11010048]{0:T(1024)(128)(4,1)} %bitcast.222), calls=%async_computation.10 | async-start | bytes 8388608
  664.8 14.6 %copy-start.5 = (bf16[384,5376,1]{1,0,2:T(8,128)(2,1)S(1)}, bf16[384,5376,1]{1,0,2:T(8,128)(2,1)}, u32[]{:S(2)}) copy-start(bf16[384,5376,1]{1,0,2:T(8,128)(2,1)} %reshape.368) | copy-start | bytes 12386308
  670.7 14.8 %collective-permute-start.6 = (bf16[384,512]{1,0:T(8,128)(2,1)}, bf16[384,512]{1,0:T(8,128)(2,1)S(1)}, u32[]{:S(2)}, u32[]{:S(2)}) collective-permute-start(bf16[384,512]{1,0:T(8,128)(2,1)} %fusion.46), channel_id=1, source_target_pairs={{0,6},{2,8},{4,10},{6,12},{8,14},{10,16},{12,18},{14,20},{16,22},{... | collective-permute-start | bytes 1179656 | tf_op jit(solution)/shard_map/ppermute | solution.py:18
  672.9 18.2 %collective-permute-start.7 = (bf16[384,512]{1,0:T(8,128)(2,1)}, bf16[384,512]{1,0:T(8,128)(2,1)}, u32[]{:S(2)}, u32[]{:S(2)}) collective-permute-start(bf16[384,512]{1,0:T(8,128)(2,1)} %fusion.46), channel_id=1, source_target_pairs={{0,4},{2,6},{4,8},{6,10},{8,12},{10,14},{12,16},{14,18},{16,20},{1... | collective-permute-start | bytes 1179656 | tf_op jit(solution)/shard_map/ppermute | solution.py:18
  677.0 14.0 %collective-permute-start.8 = (bf16[384,512]{1,0:T(8,128)(2,1)}, bf16[384,512]{1,0:T(8,128)(2,1)}, u32[]{:S(2)}, u32[]{:S(2)}) collective-permute-start(bf16[384,512]{1,0:T(8,128)(2,1)} %fusion.46), channel_id=1, source_target_pairs={{0,2},{2,4},{4,6},{6,8},{8,10},{10,12},{12,14},{14,16},{16,18},{18... | collective-permute-start | bytes 1179656 | tf_op jit(solution)/shard_map/ppermute | solution.py:18
  679.3 5.9 copy-start.20
  685.6 3.3 copy-start.9
  685.6 8.7 %collective-permute-start.11 = (bf16[384,512]{0,1:T(8,128)(2,1)}, bf16[384,512]{0,1:T(8,128)(2,1)}, u32[]{:S(2)}, u32[]{:S(2)}) collective-permute-start(bf16[384,512]{0,1:T(8,128)(2,1)} %bitcast.51), channel_id=1, source_target_pairs={{0,2},{2,4},{4,6},{6,8},{8,10},{10,12},{12,14},{14,16},{16,18},{18... | collective-permute-start | bytes 1179656 | tf_op jit(solution)/shard_map/ppermute | solution.py:18
  688.9 2.1 copy-start.10
  694.2 12.3 %copy-start.7 = (bf16[1536,512]{0,1:T(8,128)(2,1)S(1)}, bf16[1536,512]{0,1:T(8,128)(2,1)}, u32[]{:S(2)}) copy-start(bf16[1536,512]{0,1:T(8,128)(2,1)} %copy.48) | copy-start | bytes 4718596
  706.6 8.8 %copy-start.14 = (s32[2688]{0:T(1024)S(1)}, s32[2688]{0:T(1024)}, u32[]{:S(2)}) copy-start(s32[2688]{0:T(1024)} %copy-done.13) | copy-start | bytes 32260
  706.6 8.8 %copy-start.25 = (s32[2,16,42]{2,1,0:T(8,128)S(1)}, s32[2,16,42]{2,1,0:T(8,128)}, u32[]{:S(2)}) copy-start(s32[2,16,42]{2,1,0:T(8,128)} %param.22) | copy-start | bytes 16132
  752.5 4.8 copy-start.23
  757.2 19.2 %copy-start = (bf16[384,2688]{1,0:T(8,128)(2,1)S(1)}, bf16[384,2688]{1,0:T(8,128)(2,1)}, u32[]{:S(2)}) copy-start(bf16[384,2688]{1,0:T(8,128)(2,1)} %add_convert_fusion.1) | copy-start | bytes 6193156
Sparse Core Ops, SparseCore 0:
  8.9 58.6 all-gather.22
  69.9 90.7 all-gather.10
  163.0 106.7 all-gather.12
  271.2 124.8 all-gather.14
  397.5 121.8 all-gather.18
  520.8 27.1 all-gather.16
  570.4 55.9 all-gather.24
  715.5 36.9 all-gather.20
